TPU v7x, 512 devices: a whole 4x4x16 slice. The times are simulated.
512 devices in a mesh: frames: 32 (over z, core), phon: 4 (over y), chap: 4 (over x).
Axes of the slice: x: 4, y: 4, z: 16, core: 2. Of those that a mesh axis runs over, the one named last changes fastest.
Arguments:
- queries: bfloat16 [65536, 512], P(('chap', 'frames')), parts along dimension 0, may hold values from -80 to 80
- keys: bfloat16 [16384, 512], P(('chap', 'phon', 'frames')), parts along dimension 0, may hold values from -7 to 7
- values: bfloat16 [16384, 512], P(('chap', 'phon', 'frames')), parts along dimension 0, may hold values from -6 to 6
- band_first: int32 [128], P(('chap', 'frames')), parts along dimension 0, may hold values from 0 to 6, as said below
- cotangent: bfloat16 [65536, 512], P(('chap', 'frames')), parts along dimension 0, may hold values from -6 to 6
Outputs:
- aligned: bfloat16 [65536, 512], P(('chap', 'frames')), parts along dimension 0
- grad_query: bfloat16 [65536, 512], P(('chap', 'frames')), parts along dimension 0
- grad_key: float32 [16384, 512], P(('chap', 'phon', 'frames')), parts along dimension 0
- grad_value: float32 [16384, 512], P(('chap', 'phon', 'frames')), parts along dimension 0
There are 4 independent parts, one for each index of `chap`. A program takes and returns all parts, laid end to end along the dimension named above; each array names one. Nothing has to cross between parts.
Inputs may be any that keep to these rules, and one draw needn't show every extreme that they name: Query tile i attends the key tiles band_first[i] to band_first[i] + 1.
All inputs are finite; a program needn't handle non-finite values.
Results may differ from a plain program's by a relative error of at most 0.022.
Values may be sent and summed in bfloat16 or wider, within the bound.
No kernel may reach another device: no remote copies, remote signals or barrier semaphores. Data moves between devices by JAX's collectives and lax.ppermute only.
A program may use at most 64 MiB of HBM per device.

v0:
```python
import jax
import jax.numpy as jnp
from jax import lax
from jax.sharding import PartitionSpec as P

TILE = 512
NBAND = 2
NEG_FILL = -1e30


def in_one_piece(arrays, axis, dim, along):
    both = jnp.concatenate(arrays, axis=along)
    result, at, finished = (lax.all_gather(both, axis, axis=dim, tiled=True), 0, [])
    for a in arrays:
        finished.append(lax.slice_in_dim(result, at, at + a.shape[along], axis=along))
        at += a.shape[along]
    return tuple(finished)


def sent_to_all(value, axis):
    length = lax.axis_size(axis)
    return lax.all_to_all(
        jnp.broadcast_to(value[None], (length, *value.shape)), axis, 0, 0, tiled=True
    )


def of_everyone(value, axis):
    return sent_to_all(value, axis).max(axis=0)


def together(arrays, axis):
    ends = [0]
    for a in arrays:
        ends.append(ends[-1] + a.size)
    total = lax.psum(jnp.concatenate([a.ravel() for a in arrays]), axis)
    return tuple((total[b:e].reshape(a.shape) for a, b, e in zip(arrays, ends, ends[1:])))


def over_copies(value, axis):
    everything = sent_to_all(value, axis)
    return jnp.sum(everything.astype(jnp.float32), axis=0)


def side_by_side(arrays, axis, dim, along):
    ends, at = ([], 0)
    for a in arrays[:-1]:
        at += a.shape[along]
        ends.append(at)
    both = jnp.concatenate(arrays, axis=along)
    return tuple(
        jnp.split(lax.psum_scatter(both, axis, scatter_dimension=dim, tiled=True), ends, axis=along)
    )


def body(queries, keys, values, band_first, cotangent):
    width = queries.shape[1]
    scale = width ** (-0.5)
    block_keys, block_values = in_one_piece((keys, values), "frames", 0, 1)
    block = block_keys.shape[0]
    first_tile = lax.axis_index("phon") * (block // TILE)
    key_tile = first_tile + jnp.arange(block, dtype=jnp.int32) // TILE
    row_first = jnp.repeat(band_first, TILE)
    allowed = (key_tile[None, :] >= row_first[:, None]) & (
        key_tile[None, :] < row_first[:, None] + NBAND
    )
    key_float = block_keys.astype(jnp.float32)
    key_sq = jnp.sum(key_float * key_float, axis=1)
    raw = (
        jnp.dot(queries, block_keys.T, preferred_element_type=jnp.float32) - 0.5 * key_sq[None, :]
    ) * scale
    scores = jnp.where(allowed, raw, NEG_FILL)
    local_max = jnp.max(scores, axis=1)
    row_max = of_everyone(local_max, "phon")
    expd = jnp.where(allowed, jnp.exp(scores - row_max[:, None]), 0.0)
    part_total = jnp.sum(expd, axis=1)
    part_out = jnp.dot(expd.astype(jnp.bfloat16), block_values, preferred_element_type=jnp.float32)
    total, summed = together((part_total, part_out), "phon")
    aligned_f = summed / total[:, None]
    lse = row_max + jnp.log(total)
    back_keys, back_values = (block_keys, block_values)
    probs = jnp.where(allowed, jnp.exp(scores - lse[:, None]), 0.0)
    d_probs = jnp.dot(cotangent, back_values.T, preferred_element_type=jnp.float32)
    delta = jnp.sum(cotangent.astype(jnp.float32) * aligned_f, axis=1)
    d_scores = probs * (d_probs - delta[:, None])
    ds_low = d_scores.astype(jnp.bfloat16)
    part_query = jnp.dot(ds_low, back_keys, preferred_element_type=jnp.float32) * scale
    grad_query = (
        over_copies(part_query.astype(jnp.bfloat16), "phon")
        .astype(jnp.float32)
        .astype(jnp.bfloat16)
    )
    column_sum = jnp.sum(d_scores, axis=0)
    part_key = (
        jnp.einsum("qk,qd->kd", ds_low, queries, preferred_element_type=jnp.float32)
        - column_sum[:, None] * back_keys.astype(jnp.float32)
    ) * scale
    part_value = jnp.einsum(
        "qk,qd->kd", probs.astype(jnp.bfloat16), cotangent, preferred_element_type=jnp.float32
    )
    grad_key, grad_value = tuple(
        (
            part.astype(jnp.float32)
            for part in side_by_side(
                (part_key.astype(jnp.bfloat16), part_value.astype(jnp.bfloat16)), "frames", 0, 1
            )
        )
    )
    return (aligned_f.astype(jnp.bfloat16), grad_query, grad_key, grad_value)


def solution(mesh):
    in_specs = (
        P(("chap", "frames"), None),
        P(("chap", "phon", "frames"), None),
        P(("chap", "phon", "frames"), None),
        P(("chap", "frames")),
        P(("chap", "frames"), None),
    )
    out_specs = (
        P(("chap", "frames"), None),
        P(("chap", "frames"), None),
        P(("chap", "phon", "frames"), None),
        P(("chap", "phon", "frames"), None),
    )
    return jax.shard_map(body, mesh=mesh, in_specs=in_specs, out_specs=out_specs, check_vma=False)
```

profile of v0, /device:TPU:28, one launch (start us, length us, event | category | flops | bytes accessed | tf_op | source)
XLA Modules:
  0.0 291.1 jit_solution(5057413454272372290)
XLA Ops:
  7.2 0.0 all-gather.2.cloned.1.call-start
  7.2 1.5 pad_maximum_fusion.2
  8.7 0.0 all-reduce.2.cloned.1.call-start
  9.4 76.9 %all-gather.2.cloned.1.call-done = bf16[1024,1024]{1,0:T(8,128)(2,1)} async-done(((bf16[32,1024]{1,0:T(8,128)(2,1)}), bf16[1024,1024]{1,0:T(8,128)(2,1)}) %all-gather.2.cloned.1.call-update) | async-done | bytes 2097168 | tf_op jit(solution)/shard_map/all_gather | solution.py:13
  86.3 1.5 fusion
  87.8 2.0 fusion.32
  89.9 7.8 %all_to_all.11 = f32[4,1,512]{2,1,0:T(1,128)S(1)} all-to-all(f32[4,1,512]{2,1,0:T(1,128)S(1)} %broadcast_in_dim.13), channel_id=1, replica_groups=mesh['frames'=32,'phon'=4,'chap'=4] {'phon'}, dimensions={0} | all-to-all | bytes 16384 | tf_op jit(solution)/shard_map/all_to_all | solution.py:22
  97.7 0.4 fusion.4
  98.1 1.2 copy-done.3
  99.3 0.9 convolution_bitcast_fusion
  100.2 0.3 copy.23
  100.5 1.1 pad_maximum_fusion.1
  101.6 0.0 all-reduce.2.cloned.1.call-update
  101.6 0.0 reduce-scatter.2.cloned.1.call-start
  101.7 57.8 %all-reduce.2.cloned.1.call-done = f32[262656]{0:T(1024)} async-done(((f32[262656]{0:T(1024)}), f32[262656]{0:T(1024)}) %all-reduce.2.cloned.1.call-update) | async-done | bytes 1050640 | tf_op jit(solution)/shard_map/psum | solution.py:35
  159.5 1.3 slice.29
  160.8 0.2 slice.25
  160.9 0.7 log_add_fusion
  161.6 2.5 convolution_convert_fusion
  164.1 1.0 multiply_reduce_fusion
  165.2 0.7 copy-done.2
  165.9 1.1 fusion.33
  167.0 0.7 fusion.3
  167.7 0.2 copy-done.7
  167.9 1.6 pad_maximum_fusion
  169.5 1.6 copy-done.5
  171.1 2.0 fusion.7
  173.0 0.2 broadcast_in_dim.15
  173.2 27.1 %all_to_all.12 = bf16[4,512,512]{2,1,0:T(8,128)(2,1)S(1)} all-to-all(bf16[4,512,512]{2,1,0:T(8,128)(2,1)S(1)} %broadcast_in_dim.15), channel_id=1, replica_groups=mesh['frames'=32,'phon'=4,'chap'=4] {'phon'}, dimensions={0} | all-to-all | bytes 4194304 | tf_op jit(solution)/shard_map/all_to_all | solution.py:22
  200.3 1.2 reduce_sum.51
  201.5 81.6 %reduce-scatter.2.cloned.1.call-done = bf16[32,1024]{1,0:T(8,128)(2,1)} async-done(((bf16[1024,1024]{1,0:T(8,128)(2,1)}), bf16[32,1024]{1,0:T(8,128)(2,1)}) %reduce-scatter.2.cloned.1.call-update) | async-done | bytes 65552 | tf_op jit(solution)/shard_map/reduce_scatter | solution.py:51
  283.2 1.4 slice_convert_fusion
  (18 shorter events, 0.1 us)
Async XLA Ops:
  7.2 80.7 %copy-start = (bf16[512,512]{1,0:T(8,128)(2,1)S(1)}, bf16[512,512]{1,0:T(8,128)(2,1)}, u32[]{:S(2)}) copy-start(bf16[512,512]{1,0:T(8,128)(2,1)} %param.5) | copy-start | bytes 1572868
  7.2 79.1 %all-gather.2.cloned.1.call-start = ((), (), s32[]{:S(2)}) async-start(), calls=%async_computation.3 | async-start | bytes 2162688 | tf_op jit(solution)/shard_map/all_gather | solution.py:13
  8.7 150.7 %all-reduce.2.cloned.1.call-start = ((), (), s32[]{:S(2)}) async-start(), calls=%async_computation.4 | async-start | bytes 2105344 | tf_op jit(solution)/shard_map/psum | solution.py:35
  89.8 10.4 %copy-start.1 = (f32[1024,512]{1,0:T(8,128)}, f32[1024,512]{1,0:T(8,128)S(1)}, u32[]{:S(2)}) copy-start(f32[1024,512]{1,0:T(8,128)S(1)} %get-tuple-element.11) | copy-start | bytes 6291460
  97.7 1.6 copy-start.3
  101.6 60.0 %copy-start.6 = (bf16[512,512]{1,0:T(8,128)(2,1)S(1)}, bf16[512,512]{1,0:T(8,128)(2,1)}, u32[]{:S(2)}) copy-start(bf16[512,512]{1,0:T(8,128)(2,1)} %param.9) | copy-start | bytes 1572868
  101.6 181.5 %reduce-scatter.2.cloned.1.call-start = ((), (), s32[]{:S(2)}) async-start(), calls=%async_computation.5 | async-start | bytes 2162688 | tf_op jit(solution)/shard_map/reduce_scatter | solution.py:51
  161.6 3.5 %copy-start.4 = (bf16[1024,1024]{1,0:T(8,128)(2,1)S(1)}, bf16[1024,1024]{1,0:T(8,128)(2,1)}, u32[]{:S(2)}) copy-start(bf16[1024,1024]{1,0:T(8,128)(2,1)} %all-gather.2.cloned.1.call-done) | copy-start | bytes 6291460
  164.1 1.8 copy-start.2
  167.0 1.0 copy-start.7
  169.5 1.6 copy-start.5
Sparse Core Ops, SparseCore 0:
  10.7 75.5 all-gather.1
  101.7 57.6 all-reduce.1
  169.6 113.4 reduce-scatter.1
where the time goes:
time: 292 us; the launch traced here: 291 us
  waiting for transfers between devices  216 us (74%)
  blocking collectives  34.9 us (12%)
  between operations  14.5 us (5%)
  other arithmetic  10.4 us (4%)
  matrix products  9.13 us (3%)
  local copies, waits for them, and re-layouts  5.67 us (2%)
    reduce_scatter x1, waiting for transfers between devices, side_by_side(): lax.psum_scatter(both, axis, scatter_dimension=dim, tiled=True)  81.6 us
    all_gather x1, waiting for transfers between devices, in_one_piece(): lax.all_gather(both, axis, axis=dim, tiled=True)  76.9 us
    psum x1, waiting for transfers between devices, together(): total = lax.psum(jnp.concatenate([a.ravel() for a in arrays]), axis)  57.8 us
    all_to_all x2, blocking collectives, sent_to_all(): lax.all_to_all(jnp.broadcast_to(value[None], (length, *value.shape)), axi...  34.9 us
  transfers between devices with their start and end apart: 3, of which 3 were waited for; matrix products, arithmetic and copies ran while one was open for 1% of the time, Pallas kernels for 0%

commit v1 on v0

--- a/solution.py
+++ b/solution.py
@@ -32,7 +32,9 @@
     ends = [0]
     for a in arrays:
         ends.append(ends[-1] + a.size)
-    total = lax.psum(jnp.concatenate([a.ravel() for a in arrays]), axis)
+    part_2 = jnp.concatenate([a.ravel() for a in arrays])
+    shards = lax.all_gather(part_2, axis)
+    total = jnp.sum(shards, axis=0)
     return tuple((total[b:e].reshape(a.shape) for a, b, e in zip(arrays, ends, ends[1:])))
 
 

time: 292 us -> 310 us (1.062)
  the two profiles are of different devices: /device:TPU:28 before, /device:TPU:24 now
where the time goes in v1:
time: 310 us; the launch traced here: 309 us
  waiting for transfers between devices  208 us (67%)
  blocking collectives  37.4 us (12%)
  other arithmetic  29.3 us (9%)
  between operations  14.6 us (5%)
  local copies, waits for them, and re-layouts  10.9 us (4%)
  matrix products  9.12 us (3%)
    reduce_scatter x1, waiting for transfers between devices, side_by_side(): lax.psum_scatter(both, axis, scatter_dimension=dim, tiled=True)  80 us
    all_gather x1, waiting for transfers between devices, in_one_piece(): lax.all_gather(both, axis, axis=dim, tiled=True)  76.9 us
    all_gather x1, waiting for transfers between devices, together(): shards = lax.all_gather(part_2, axis)  51 us
    all_to_all x2, blocking collectives, sent_to_all(): lax.all_to_all(jnp.broadcast_to(value[None], (length, *value.shape)), axi...  37.4 us
    reduce_sum x1, other arithmetic, together(): total = jnp.sum(shards, axis=0)  20.5 us
    unnamed x18, local copies, waits for them, and re-layouts  10.5 us
  transfers between devices with their start and end apart: 3, of which 3 were waited for; matrix products, arithmetic and copies ran while one was open for 1% of the time, Pallas kernels for 0%

profile of v1, /device:TPU:24, one launch (start us, length us, event | category | flops | bytes accessed | tf_op | source)
XLA Modules:
  0.0 309.4 jit_solution(17585557859611757439)
XLA Ops:
  7.2 1.5 pad_maximum_fusion.2
  8.7 0.0 all-gather.7.cloned.1.call-start
  9.4 76.9 %all-gather.5.cloned.1.call-done = bf16[1024,1024]{1,0:T(8,128)(2,1)} async-done(((bf16[32,1024]{1,0:T(8,128)(2,1)}), bf16[1024,1024]{1,0:T(8,128)(2,1)}) %all-gather.5.cloned.1.call-update) | async-done | bytes 2097168 | tf_op jit(solution)/shard_map/all_gather | solution.py:13
  86.4 1.5 fusion
  87.9 2.0 fusion.32
  89.9 7.8 %all_to_all.11 = f32[4,1,512]{2,1,0:T(1,128)S(1)} all-to-all(f32[4,1,512]{2,1,0:T(1,128)S(1)} %broadcast_in_dim.13), channel_id=1, replica_groups=mesh['frames'=32,'phon'=4,'chap'=4] {'phon'}, dimensions={0} | all-to-all | bytes 16384 | tf_op jit(solution)/shard_map/all_to_all | solution.py:22
  97.8 0.4 fusion.4
  98.2 1.2 copy-done.3
  99.4 0.9 convolution_bitcast_fusion
  100.3 0.3 copy.26
  100.5 0.1 pad_maximum_fusion.1
  100.6 5.7 %reshape.53 = f32[1,1,262656]{2,1,0:T(1,128)} reshape(f32[262656]{0:T(1024)S(1)} %pad_maximum_fusion.1) | data formatting | bytes 2101248
  106.3 0.0 reduce-scatter.2.cloned.1.call-start
  106.4 51.0 %all-gather.7.cloned.1.call-done = f32[4,1,262656]{2,1,0:T(1,128)} async-done(((f32[1,1,262656]{2,1,0:T(1,128)}), f32[4,1,262656]{2,1,0:T(1,128)}) %all-gather.7.cloned.1.call-update) | async-done | bytes 4202512 | tf_op jit(solution)/shard_map/all_gather | solution.py:36
  157.3 20.5 %reduce_sum.59 = f32[262656]{0:T(1024)S(1)} reduce(f32[4,1,262656]{2,1,0:T(1,128)} %all-gather.7.cloned.1.call-done, f32[]{:T(128)} %constant.34.clone.1), dimensions={0,1}, to_apply=%region_4.5 | reduce | flops 787968 | bytes 5253124 | tf_op jit(solution)/shard_map/reduce_sum | solution.py:37
  177.9 0.1 slice.29
  178.0 0.2 slice.25
  178.2 0.8 copy-done.6
  178.9 2.5 convolution_convert_fusion
  181.5 1.0 multiply_reduce_fusion
  182.5 0.7 copy-done.2
  183.2 1.1 fusion.33
  184.3 0.7 fusion.3
  185.0 0.3 copy-done.7
  185.3 1.6 pad_maximum_fusion
  186.9 1.6 copy-done.5
  188.5 2.0 fusion.7
  190.4 0.2 broadcast_in_dim.15
  190.6 29.6 %all_to_all.12 = bf16[4,512,512]{2,1,0:T(8,128)(2,1)S(1)} all-to-all(bf16[4,512,512]{2,1,0:T(8,128)(2,1)S(1)} %broadcast_in_dim.15), channel_id=1, replica_groups=mesh['frames'=32,'phon'=4,'chap'=4] {'phon'}, dimensions={0} | all-to-all | bytes 4194304 | tf_op jit(solution)/shard_map/all_to_all | solution.py:22
  220.2 1.2 reduce_sum.61
  221.4 80.0 %reduce-scatter.2.cloned.1.call-done = bf16[32,1024]{1,0:T(8,128)(2,1)} async-done(((bf16[1024,1024]{1,0:T(8,128)(2,1)}), bf16[32,1024]{1,0:T(8,128)(2,1)}) %reduce-scatter.2.cloned.1.call-update) | async-done | bytes 65552 | tf_op jit(solution)/shard_map/reduce_scatter | solution.py:53
  301.4 1.4 slice_convert_fusion
  (20 shorter events, 0.2 us)
Async XLA Ops:
  7.2 80.7 %copy-start = (bf16[512,512]{1,0:T(8,128)(2,1)S(1)}, bf16[512,512]{1,0:T(8,128)(2,1)}, u32[]{:S(2)}) copy-start(bf16[512,512]{1,0:T(8,128)(2,1)} %param.5) | copy-start | bytes 1572868
  7.2 79.2 %all-gather.5.cloned.1.call-start = ((), (), s32[]{:S(2)}) async-start(), calls=%async_computation.3 | async-start | bytes 2162688 | tf_op jit(solution)/shard_map/all_gather | solution.py:13
  8.7 148.6 %all-gather.7.cloned.1.call-start = ((), (), s32[]{:S(2)}) async-start(), calls=%async_computation.5 | async-start | bytes 5253120 | tf_op jit(solution)/shard_map/all_gather | solution.py:36
  89.9 10.4 %copy-start.1 = (f32[1024,512]{1,0:T(8,128)}, f32[1024,512]{1,0:T(8,128)S(1)}, u32[]{:S(2)}) copy-start(f32[1024,512]{1,0:T(8,128)S(1)} %get-tuple-element.11) | copy-start | bytes 6291460
  97.8 1.6 copy-start.3
  106.3 195.1 %reduce-scatter.2.cloned.1.call-start = ((), (), s32[]{:S(2)}) async-start(), calls=%async_computation.4 | async-start | bytes 2162688 | tf_op jit(solution)/shard_map/reduce_scatter | solution.py:53
  177.9 1.0 copy-start.6
  178.9 3.5 %copy-start.4 = (bf16[1024,1024]{1,0:T(8,128)(2,1)S(1)}, bf16[1024,1024]{1,0:T(8,128)(2,1)}, u32[]{:S(2)}) copy-start(bf16[1024,1024]{1,0:T(8,128)(2,1)} %all-gather.5.cloned.1.call-done) | copy-start | bytes 6291460
  181.4 1.8 copy-start.2
  184.3 1.0 copy-start.7
  186.9 1.6 copy-start.5
Sparse Core Ops, SparseCore 0:
  10.7 75.6 all-gather.4
  106.4 50.8 all-gather.6
  187.0 114.3 reduce-scatter.1
